TPU v7x, 32 devices: a whole 2x2x4 slice. The times are simulated.
32 devices in a mesh: state: 8 (over z, y), tile: 4 (over x, core).
Axes of the slice: x: 2, y: 2, z: 4, core: 2. Of those that a mesh axis runs over, the one named last changes fastest.
Arguments:
- pair_tiles: bfloat16 [8, 4, 64, 64, 128], P('state', 'tile'), may hold values from -60 to 60
- targets: int32 [8, 4, 16, 2, 128], P('state', 'tile'), may hold values from 0 to 63, as said below
- offsets: int32 [8], replicated, may hold values from 0 to 128, as said below
- ln_gain: float32 [128], replicated, may hold values from 0.5 to 1.5
- ln_bias: float32 [128], replicated, may hold values from -3 to 3
- w_query: bfloat16 [128, 128], replicated, may hold values from -0.5 to 0.5
- w_key: bfloat16 [128, 128], replicated, may hold values from -0.5 to 0.5
- w_value: bfloat16 [128, 128], replicated, may hold values from -0.5 to 0.5
- w_pairbias: float32 [128, 4], replicated, may hold values from -25 to 25
- w_gate: bfloat16 [128, 128], replicated, may hold values from -0.5 to 0.5
- gate_bias: float32 [128], replicated, may hold values from -4 to 4
- w_output: bfloat16 [128, 128], replicated, may hold values from -0.5 to 0.5
- out_bias: float32 [128], replicated, may hold values from -3 to 3
- w_distogram: float32 [128, 64], replicated, may hold values from -4 to 4
- dist_bias: float32 [64], replicated, may hold values from -4 to 4
Outputs:
- shared_grad: float32 [4, 4, 16, 2, 128, 128], P(None, 'tile', None, None, 'state')
Inputs may be any that keep to these rules, and one draw needn't show every extreme that they name: `targets`: symmetric: the bin of crop pair (x, y) equals that of (y, x) in every state. `offsets`: each is a multiple of 64; some state starts at 0 and some state at 128.
All inputs are finite; a program needn't handle non-finite values.
Results may differ from a plain program's by a relative error of at most 0.015.
Values may be sent and summed in bfloat16 or wider, within the bound.
No kernel may reach another device: no remote copies, remote signals or barrier semaphores. Data moves between devices by JAX's collectives and lax.ppermute only.
A program may use at most 64 MiB of HBM per device.

v0:
```python
import math
import jax
import jax.numpy as jnp
from jax import lax
from jax.sharding import PartitionSpec as P

C = 128
H = 4
HD = 32
NB = 64
L = 128


def layer_norm(pair_field, ln_gain, ln_bias):
    center = pair_field - jnp.mean(pair_field, axis=-1, keepdims=True)
    inverse = lax.rsqrt(jnp.mean(center * center, axis=-1, keepdims=True) + 1e-05)
    normed = center * inverse
    return (normed * ln_gain + ln_bias, normed, inverse)


def probabilities(queries, key_proj, bias_full):
    scores = jnp.einsum("rjhd,rkhd->rhjk", queries, key_proj, preferred_element_type=jnp.float32)
    scores = scores * (1.0 / math.sqrt(HD)) + bias_full[None]
    row_max = jnp.max(scores, axis=-1, keepdims=True)
    exp_scores = jnp.exp(scores - row_max)
    return exp_scores / jnp.sum(exp_scores, axis=-1, keepdims=True)


def on_device(
    pair_tiles,
    targets,
    offsets,
    ln_gain,
    ln_bias,
    w_query,
    w_key,
    w_value,
    w_pairbias,
    w_gate,
    gate_bias,
    w_output,
    out_bias,
    w_distogram,
    dist_bias,
):
    tile_count = lax.axis_size("tile")
    state_count = lax.axis_size("state")
    tile_side = pair_tiles.shape[2]
    tile_grid = L // tile_side
    row_share = tile_side // tile_count
    rows_here = row_share * tile_grid
    hidden_width = H * HD
    inv_root = 1.0 / math.sqrt(HD)
    block_rows = 2
    groups = rows_here // block_rows

    def split_rows(values_in):
        return values_in.reshape((groups, block_rows) + values_in.shape[1:])

    blocked = pair_tiles[0, 0].reshape(tile_count, row_share, tile_side, C)
    regrouped = lax.all_to_all(blocked, "tile", split_axis=0, concat_axis=2, tiled=True)
    pair_field = regrouped.reshape(rows_here, L, C).astype(jnp.float32)
    normed_out, normed, inverse = layer_norm(pair_field, ln_gain, ln_bias)
    flat_b = normed_out.astype(jnp.bfloat16).reshape(rows_here * L, C)

    def project(weight):
        return (
            jnp.dot(flat_b, weight, preferred_element_type=jnp.float32)
            .astype(jnp.bfloat16)
            .reshape(rows_here, L, H, HD)
        )

    queries = project(w_query)
    key_proj = project(w_key)
    value_proj = project(w_value)
    gate_act = jax.nn.sigmoid(
        jnp.dot(flat_b, w_gate, preferred_element_type=jnp.float32) + gate_bias
    ).reshape(rows_here, L, hidden_width)
    bias_rows = jnp.einsum("rlc,ch->hrl", normed_out, w_pairbias, precision=lax.Precision.HIGHEST)
    gathered = lax.all_gather(bias_rows, "tile", axis=1, tiled=True)
    bias_full = (
        gathered.reshape(H, tile_count, row_share, tile_grid, L)
        .transpose(0, 3, 1, 2, 4)
        .reshape(H, L, L)
    )

    def forward_block(block_args):
        query_blk, key_blk, value_blk = block_args
        weights_b = probabilities(query_blk, key_blk, bias_full).astype(jnp.bfloat16)
        return jnp.einsum(
            "rhjk,rkhd->rjhd", weights_b, value_blk, preferred_element_type=jnp.float32
        )

    attended = lax.map(
        forward_block, (split_rows(queries), split_rows(key_proj), split_rows(value_proj))
    ).reshape(rows_here, L, hidden_width)
    gated_out = (gate_act * attended).astype(jnp.bfloat16)
    updated = (
        pair_field
        + jnp.dot(
            gated_out.reshape(rows_here * L, hidden_width),
            w_output,
            preferred_element_type=jnp.float32,
        ).reshape(rows_here, L, C)
        + out_bias
    )
    outgoing = updated.reshape(row_share, tile_grid, tile_grid, tile_count, row_share * C)
    incoming = lax.all_to_all(
        outgoing.astype(jnp.bfloat16), "tile", split_axis=3, concat_axis=3, tiled=True
    ).astype(outgoing.dtype)
    mirrored = (
        incoming.reshape(row_share, tile_grid, tile_grid, tile_count, row_share, C)
        .transpose(4, 2, 1, 3, 0, 5)
        .reshape(rows_here, L, C)
    )
    logits = (
        jnp.einsum("rlc,cb->rlb", updated + mirrored, w_distogram, precision=lax.Precision.HIGHEST)
        + dist_bias
    )
    row_max = jnp.max(logits, axis=-1, keepdims=True)
    exp_logits = jnp.exp(logits - row_max)
    bin_prob = exp_logits / jnp.sum(exp_logits, axis=-1, keepdims=True)
    target_here = targets.reshape(rows_here, L)
    onehot = (target_here[:, :, None] == jnp.arange(NB, dtype=jnp.int32)[None, None, :]).astype(
        jnp.float32
    )
    logit_grad = 2.0 * (bin_prob - onehot)
    pair_grad = jnp.einsum("rlb,cb->rlc", logit_grad, w_distogram, precision=lax.Precision.HIGHEST)
    out_grad = jnp.einsum(
        "rlc,wc->rlw", pair_grad.astype(jnp.bfloat16), w_output, preferred_element_type=jnp.float32
    )
    att_grad_b = (out_grad * gate_act).astype(jnp.bfloat16).reshape(rows_here, L, H, HD)
    gate_grad = out_grad * attended * gate_act * (1.0 - gate_act)

    def backward_block(bias_sum, block_args):
        query_blk, key_blk, value_blk, grad_blk = block_args
        attn_prob = probabilities(query_blk, key_blk, bias_full)
        weights_b = attn_prob.astype(jnp.bfloat16)
        value_grad = jnp.einsum(
            "rhjk,rjhd->rkhd", weights_b, grad_blk, preferred_element_type=jnp.float32
        )
        weight_grad = jnp.einsum(
            "rjhd,rkhd->rhjk", grad_blk, value_blk, preferred_element_type=jnp.float32
        )
        score_grad = attn_prob * (
            weight_grad - jnp.sum(attn_prob * weight_grad, axis=-1, keepdims=True)
        )
        score_b = score_grad.astype(jnp.bfloat16)
        query_grad = (
            jnp.einsum("rhjk,rkhd->rjhd", score_b, key_blk, preferred_element_type=jnp.float32)
            * inv_root
        )
        key_grad = (
            jnp.einsum("rhjk,rjhd->rkhd", score_b, query_blk, preferred_element_type=jnp.float32)
            * inv_root
        )
        return (bias_sum + jnp.sum(score_grad, axis=0), (query_grad, key_grad, value_grad))

    bias_grad, grad_parts = lax.scan(
        backward_block,
        jnp.zeros((H, L, L), jnp.float32),
        (split_rows(queries), split_rows(key_proj), split_rows(value_proj), split_rows(att_grad_b)),
    )
    query_grad, key_grad, value_grad = grad_parts
    owner_order = (
        bias_grad.reshape(H, tile_grid, tile_count, row_share, L)
        .transpose(0, 2, 3, 1, 4)
        .reshape(H, L, L)
    )
    bias_share = lax.psum_scatter(
        owner_order.astype(jnp.bfloat16), "tile", scatter_dimension=1, tiled=True
    ).astype(jnp.float32)

    def back_project(grad_part, weight):
        return jnp.einsum(
            "rlw,cw->rlc",
            grad_part.reshape(rows_here, L, hidden_width).astype(jnp.bfloat16),
            weight,
            preferred_element_type=jnp.float32,
        )

    normed_grad = (
        back_project(query_grad, w_query)
        + back_project(key_grad, w_key)
        + back_project(value_grad, w_value)
        + back_project(gate_grad, w_gate)
    )
    normed_grad = normed_grad + jnp.einsum(
        "hrl,ch->rlc", bias_share, w_pairbias, precision=lax.Precision.HIGHEST
    )
    scaled = normed_grad * ln_gain
    ln_back = inverse * (
        scaled
        - jnp.mean(scaled, axis=-1, keepdims=True)
        - normed * jnp.mean(scaled * normed, axis=-1, keepdims=True)
    )
    total_grad = (pair_grad + ln_back).astype(jnp.bfloat16)
    state_here = lax.axis_index("state")
    piece_cols = L // state_count
    shifted = jnp.roll(total_grad, offsets[state_here], axis=1)
    outgoing_rows = shifted.reshape(rows_here, state_count, piece_cols, C)
    received = lax.all_to_all(outgoing_rows, "state", split_axis=1, concat_axis=1, tiled=True)
    placed = (
        received.astype(jnp.float32)
        .reshape(row_share, tile_grid, state_count, piece_cols, C)
        .transpose(2, 1, 0, 3, 4)
    )
    columns = state_here * piece_cols + jnp.arange(piece_cols, dtype=jnp.int32)
    full_blocks = 2 * tile_grid

    def place(source, accum):
        offset = offsets[source]
        high_half = (columns < offset).astype(jnp.float32)[:, None]
        incoming_blk = lax.dynamic_index_in_dim(placed, source, 0, keepdims=False)
        contrib = jnp.stack([incoming_blk * (1.0 - high_half), incoming_blk * high_half], axis=2)
        row_start = offset // tile_side
        zero_index = jnp.zeros((), jnp.int32)
        corner = (row_start, zero_index, zero_index, zero_index, zero_index)
        window = lax.dynamic_slice(accum, corner, contrib.shape)
        return lax.dynamic_update_slice(accum, window + contrib, corner)

    accum = lax.fori_loop(
        0, state_count, place, jnp.zeros((full_blocks, row_share, 2, piece_cols, C), jnp.float32)
    )
    return accum.reshape(full_blocks, 1, row_share, 2, piece_cols, C)


def solution(mesh):
    in_specs = (
        P("state", "tile", None, None, None),
        P("state", "tile", None, None, None),
        P(),
        P(),
        P(),
        P(),
        P(),
        P(),
        P(),
        P(),
        P(),
        P(),
        P(),
        P(),
        P(),
    )
    out_specs = P(None, "tile", None, None, "state", None)
    return jax.shard_map(
        on_device, mesh=mesh, in_specs=in_specs, out_specs=out_specs, check_vma=False
    )
```

profile of v0, /device:TPU:0, one launch (start us, length us, event | category | flops | bytes accessed | tf_op | source)
XLA Modules:
  0.0 457.8 jit_solution(5351371893127979779)
XLA Ops:
  6.5 4.4 all-to-all-start
  10.9 14.4 %all-to-all-done = bf16[4,16,64,128]{3,2,1,0:T(8,128)(2,1)S(1)} async-done(((bf16[4,16,64,128]{3,2,1,0:T(8,128)(2,1)}), bf16[4,16,64,128]{3,2,1,0:T(8,128)(2,1)S(1)}, u32[]{:S(2)}, u32[]{:S(2)}) %all-to-all-start) | async-done | bytes 1048608 | tf_op jit(solution)/shard_map/all_to_all | solution.py:61
  28.0 3.2 fusion.100
  31.2 5.8 %all_gather.3 = f32[4,128,128]{2,0,1:T(4,128)S(1)} all-gather(f32[4,32,128]{2,0,1:T(4,128)S(1)} %fusion.100), channel_id=1, replica_groups=mesh['state'=8,'tile'=4] {'tile'}, dimensions={1}, use_global_device_ids=true | all-gather | bytes 327680 | tf_op jit(solution)/shard_map/all_gather | solution.py:80
  41.0 2.7 reshape_reshape.15
  43.7 2.6 copy.165
  47.7 2.3 copy.162
  50.0 2.6 reshape_reshape.16
  52.6 2.7 copy.166
  59.6 2.6 copy.167
  62.2 68.6 %while.46 = (s32[]{:T(128)}, f32[16,2,128,4,32]{2,4,3,1,0:T(8,128)}, bf16[16,2,128,4,32]{2,4,3,1,0:T(8,128)(2,1)}, bf16[16,2,128,4,32]{2,4,3,1,0:T(8,128)(2,1)},...) while((s32[]{:T(128)}, f32[16,2,128,4,32]{2,4,3,1,0:T(8,128)}, ...), condition=%wide.region_5.6_spmd.clone, body=%wide.region_2.5_spmd.sunk.clone | while | flops 26346752 | bytes 3091525 | solution.py:94
  130.8 4.5 copy.168
  135.3 3.9 reshape.172
  139.3 3.0 copy.169
  142.3 3.7 multiply_convert_fusion.2
  148.9 2.8 copy.170
  151.7 3.5 all-to-all-start.1
  161.9 2.9 copy.173
  164.8 4.8 %all-to-all-done.1 = bf16[16,2,2,4,2048]{4,0,2,1,3:T(8,128)(2,1)S(1)} async-done(((bf16[16,2,2,4,2048]{4,0,2,1,3:T(8,128)(2,1)}), bf16[16,2,2,4,2048]{4,0,2,1,3:T(8,128)(2,1)S(1)}, u32[]{:S(2)}, u32[]{:S(2)}) %all-to-all-start.1) | async-done | bytes 1048608 | tf_op jit(solution)/shard_map/all_to_all | solution.py:108
  171.8 2.4 fusion.97
  175.7 3.5 fusion.108
  179.2 2.3 multiply_convert_fusion.1
  181.5 155.2 %while.48 = (s32[]{:T(128)}, f32[4,128,128]{1,2,0:T(8,128)}, bf16[16,2,128,4,32]{2,4,3,1,0:T(8,128)(2,1)}, bf16[16,2,128,4,32]{2,4,3,1,0:T(8,128)(2,1)}, bf16[16...) while((s32[]{:T(128)}, f32[4,128,128]{1,2,0:T(8,128)}, ...), condition=%wide.region_13.14_spmd.clone.clone, body=%wide.region_8.13_spmd.clone.sunk.clone | while | flops 52691200 | bytes 6518895 | solution.py:159
  315.2 2.1 fusion.244
  336.7 3.1 fusion.122
  342.8 4.8 %fusion.103 = f32[32,128,128]{2,1,0:T(8,128)} fusion(f32[32,128,128]{1,2,0:T(8,128)} %copy.173, f32[32,128,128]{1,2,0:T(8,128)} %get-tuple-element.441, f32[32,128,128]{1,2,0:T(8,128)} %bitcast.299, bf16[128,128]{1,0:T(8,128)(2,1)S(1)} %copy-done.19), kind=kOutput, calls=%fused_computation.110 | convolution fusion | flops 136839168 | bytes 8421376 | tf_op jit(solution)/shard_map/rlw,cw->rlc/dot_general | solution.py:175
  349.3 26.4 %all-reduce.3.cloned.1.call-done = bf16[4,128,128]{2,0,1:T(4,128)(2,1)} async-done(((bf16[4,128,128]{2,0,1:T(4,128)(2,1)}), bf16[4,128,128]{2,0,1:T(4,128)(2,1)}) %all-reduce.3.cloned.1.call-update) | async-done | bytes 131088
  375.7 5.9 %fusion.137 = (f32[32,128]{1,0:T(8,128)S(1)}, f32[32,128]{1,0:T(8,128)S(1)}, f32[32,128,128]{2,1,0:T(8,128)S(1)}) fusion(f32[32,128]{1,0:T(8,128)S(1)} %rsqrt.17, f32[32,128,128]{2,1,0:T(8,128)S(1)} %bitcast.290, f32[32,128]{1,0:T(8,128)S(1)} %div.57, f32[128]{0:T(128)S(1)} %copy-done.21, f32[128,4]{0,1:T(4,128)S(1)} %copy-done.20, ...), kind=kOutput, calls=%fused_computation.151 | convolution fusion | flops 30400512 | bytes 12683780 | tf_op jit(solution)/shard_map/hrl,ch->rlc/dot_general | solution.py:188
  381.6 2.5 add_convert_fusion
  386.0 5.5 %all-to-all-start.2 = ((bf16[32,8,16,128]{3,2,0,1:T(8,128)(2,1)}), bf16[32,8,16,128]{3,2,0,1:T(8,128)(2,1)S(1)}, u32[]{:S(2)}, u32[]{:S(2)}) async-start(bf16[32,8,16,128]{3,2,0,1:T(8,128)(2,1)} %copy.191), calls=%async_computation.2 | async-start | bytes 2097152 | tf_op jit(solution)/shard_map/all_to_all | solution.py:202
  391.6 24.9 %all-to-all-done.2 = bf16[32,8,16,128]{3,2,0,1:T(8,128)(2,1)S(1)} async-done(((bf16[32,8,16,128]{3,2,0,1:T(8,128)(2,1)}), bf16[32,8,16,128]{3,2,0,1:T(8,128)(2,1)S(1)}, u32[]{:S(2)}, u32[]{:S(2)}) %all-to-all-start.2) | async-done | bytes 1048608 | tf_op jit(solution)/shard_map/all_to_all | solution.py:202
  417.2 32.8 %while.47 = (s32[]{:T(128)}, f32[4,16,2,16,128]{4,3,2,1,0:T(8,128)S(1)}, s32[8]{0:T(128)S(1)}, f32[8,2,16,16,128]{4,3,0,1,2:T(8,128)S(1)}, s32[]{:T(128)}) while((s32[]{:T(128)}, f32[4,16,2,16,128]{4,3,2,1,0:T(8,128)S(1)}, s32[8]{0:T(128)S(1)}, f32[8,2,16,16,128]{4,3,0,1,2:T(8,128)S(1)}, s32[]{:T(128)}) %tuple.139), condition=%wide.region_18.19_spmd.clone.clone, body=%wide.region_17.18_spmd.clone.sunk.clone | while | flops 393300 | bytes 2360721 | solution.py:222
  (324 shorter events, 264.0 us)
Async XLA Ops:
  6.5 139.5 %copy-start = (bf16[128,128]{1,0:T(8,128)(2,1)S(1)}, bf16[128,128]{1,0:T(8,128)(2,1)}, u32[]{:S(2)}) copy-start(bf16[128,128]{1,0:T(8,128)(2,1)} %param.32) | copy-start | bytes 98308
  6.5 18.8 %all-to-all-start = ((bf16[4,16,64,128]{3,2,1,0:T(8,128)(2,1)}), bf16[4,16,64,128]{3,2,1,0:T(8,128)(2,1)S(1)}, u32[]{:S(2)}, u32[]{:S(2)}) async-start(bf16[4,16,64,128]{3,2,1,0:T(8,128)(2,1)} %bitcast.308), calls=%async_computation | async-start | bytes 2097152 | tf_op jit(solution)/shard_map/all_to_all | solution.py:61
  26.1 1.9 copy-start.20
  26.1 1.9 copy-start.21
  26.1 1.9 copy-start.22
  28.0 11.3 %copy-start.14 = (bf16[128,128]{1,0:T(8,128)(2,1)S(1)}, bf16[128,128]{1,0:T(8,128)(2,1)}, u32[]{:S(2)}) copy-start(bf16[128,128]{1,0:T(8,128)(2,1)} %param.28) | copy-start | bytes 98308
  38.3 1.0 copy-start.5
  41.0 5.3 %copy-start.6 = (bf16[4096,128]{1,0:T(8,128)(2,1)S(1)}, bf16[4096,128]{1,0:T(8,128)(2,1)}, u32[]{:S(2)}) copy-start(bf16[4096,128]{1,0:T(8,128)(2,1)} %copy-done.5) | copy-start | bytes 3145732
  41.0 5.3 %copy-start.16 = (bf16[128,128]{1,0:T(8,128)(2,1)S(1)}, bf16[128,128]{1,0:T(8,128)(2,1)}, u32[]{:S(2)}) copy-start(bf16[128,128]{1,0:T(8,128)(2,1)} %param.26) | copy-start | bytes 98308
  50.0 5.2 %copy-start.15 = (bf16[128,128]{1,0:T(8,128)(2,1)S(1)}, bf16[128,128]{1,0:T(8,128)(2,1)}, u32[]{:S(2)}) copy-start(bf16[128,128]{1,0:T(8,128)(2,1)} %param.27) | copy-start | bytes 98308
  139.3 3.0 copy-start.7
  139.3 3.0 copy-start.26
  142.3 3.7 copy-start.23
  151.7 17.9 %all-to-all-start.1 = ((bf16[16,2,2,4,2048]{4,0,2,1,3:T(8,128)(2,1)}), bf16[16,2,2,4,2048]{4,0,2,1,3:T(8,128)(2,1)S(1)}, u32[]{:S(2)}, u32[]{:S(2)}) async-start(bf16[16,2,2,4,2048]{4,0,2,1,3:T(8,128)(2,1)} %copy.170), calls=%async_computation.1 | async-start | bytes 2097152 | tf_op jit(solution)/shard_map/all_to_all | solution.py:108
  155.2 220.5 %all-reduce.3.cloned.1.call-start = ((), (), s32[]{:S(2)}) async-start(), calls=%async_computation.3 | async-start | bytes 262144
  155.7 1.3 copy-start.3
  155.7 2.4 copy-start.27
  155.7 4.9 %copy-start.28 = (u32[32]{0:T(128)S(1)}, u32[32]{0:T(128)}, u32[]{:S(2)}) copy-start(u32[32]{0:T(128)} %constant.184) | copy-start | bytes 388
  170.2 1.6 copy-start.12
  170.2 1.6 copy-start.18
  170.3 1.6 copy-start.24
  174.2 1.5 copy-start.25
  175.7 3.5 copy-start.2
  179.2 2.3 copy-start.10
  336.7 3.1 copy-start.13
  339.9 1.8 copy-start.9
  339.9 2.9 copy-start.19
  342.7 4.8 %copy-start.4 = (bf16[16,2,128,4,32]{2,4,3,1,0:T(8,128)(2,1)S(1)}, bf16[16,2,128,4,32]{2,4,3,1,0:T(8,128)(2,1)}, u32[]{:S(2)}) copy-start(bf16[16,2,128,4,32]{2,4,3,1,0:T(8,128)(2,1)} %get-tuple-element.226) | copy-start | bytes 3145732
  342.7 4.8 %copy-start.17 = (bf16[128,128]{1,0:T(8,128)(2,1)S(1)}, bf16[128,128]{1,0:T(8,128)(2,1)}, u32[]{:S(2)}) copy-start(bf16[128,128]{1,0:T(8,128)(2,1)} %param.26) | copy-start | bytes 98308
  375.7 5.9 %copy-start.11 = (f32[32,128,128]{2,1,0:T(8,128)S(1)}, f32[32,128,128]{2,1,0:T(8,128)}, u32[]{:S(2)}) copy-start(f32[32,128,128]{2,1,0:T(8,128)} %copy-done.10) | copy-start | bytes 6291460
  386.0 30.4 %all-to-all-start.2 = ((bf16[32,8,16,128]{3,2,0,1:T(8,128)(2,1)}), bf16[32,8,16,128]{3,2,0,1:T(8,128)(2,1)S(1)}, u32[]{:S(2)}, u32[]{:S(2)}) async-start(bf16[32,8,16,128]{3,2,0,1:T(8,128)(2,1)} %copy.191), calls=%async_computation.2 | async-start | bytes 2097152 | tf_op jit(solution)/shard_map/all_to_all | solution.py:202
  450.0 1.0 copy-start.8
  (1 other events, 1.0 us)
Sparse Core Ops, SparseCore 0:
  342.8 32.8 all-reduce.2
where the time goes:
time: 466 us; the launch traced here: 458 us
  matrix products  229 us (49%)
  waiting for transfers between devices  70.6 us (15%)
  local copies, waits for them, and re-layouts  57.3 us (12%)
  other arithmetic  43.7 us (9%)
  loops' own time  21.7 us (5%)
  between operations  16.4 us (4%)
  starting transfers between devices  13.6 us (3%)
  blocking collectives  5.78 us (1%)
    sub x32, matrix products, probabilities(): exp_scores = jnp.exp(scores - row_max)  40.1 us
    dot_general x16, matrix products, backward_block(): jnp.einsum('rhjk,rjhd->rkhd', weights_b, grad_blk, preferred_element_type...  32.6 us
    dot_general x16, matrix products, forward_block(): jnp.einsum('rhjk,rkhd->rjhd', weights_b, value_blk, preferred_element_typ...  27.8 us
    dot_general x16, matrix products, backward_block(): jnp.einsum('rhjk,rjhd->rkhd', score_b, query_blk, preferred_element_type=...  27.3 us
    unnamed x2, waiting for transfers between devices  26.4 us
    dot_general x16, matrix products, backward_block(): jnp.einsum('rhjk,rkhd->rjhd', score_b, key_blk, preferred_element_type=jn...  26.4 us
    add x16, other arithmetic, backward_block(): bias_sum + jnp.sum(score_grad, axis=0)  25.9 us
    all_to_all x1, waiting for transfers between devices, on_device(): lax.all_to_all(outgoing_rows, 'state', split_axis=1, concat_axis=1, tiled...  24.9 us
  transfers between devices with their start and end apart: 4, of which 4 were waited for; matrix products, arithmetic and copies ran while one was open for 3% of the time, Pallas kernels for 0%

commit v1 on v0

--- a/solution.py
+++ b/solution.py
@@ -9,6 +9,18 @@
 HD = 32
 NB = 64
 L = 128
+
+
+def rotated_exchange(array, axis, split, join):
+    ways, here = (lax.axis_size(axis), lax.axis_index(axis))
+    width = array.shape[split] // ways
+    turned = jnp.roll(array, -here * width, axis=split)
+    got = [lax.slice_in_dim(turned, 0, width, axis=split)]
+    for far in range(1, ways):
+        sent = lax.slice_in_dim(turned, far * width, (far + 1) * width, axis=split)
+        got.append(lax.ppermute(sent, axis, [(d, (d + far) % ways) for d in range(ways)]))
+    line = jnp.concatenate(got[::-1], axis=join)
+    return jnp.roll(line, (here + 1) * got[0].shape[join], axis=join)
 
 
 def layer_norm(pair_field, ln_gain, ln_bias):
@@ -199,7 +211,7 @@
     piece_cols = L // state_count
     shifted = jnp.roll(total_grad, offsets[state_here], axis=1)
     outgoing_rows = shifted.reshape(rows_here, state_count, piece_cols, C)
-    received = lax.all_to_all(outgoing_rows, "state", split_axis=1, concat_axis=1, tiled=True)
+    received = rotated_exchange(outgoing_rows, "state", 1, 1)
     placed = (
         received.astype(jnp.float32)
         .reshape(row_share, tile_grid, state_count, piece_cols, C)

time: 466 us -> 459 us (0.985)
  waiting for transfers between devices: 70.6 us -> 63.3 us
    all_to_all x1 -> x0, waiting for transfers between devices: 24.9 us -> none  [on_device(): lax.all_to_all(outgoing_rows, 'state', split_axis=1, concat_axis=1, tiled...]
    ppermute x0 -> x7, waiting for transfers between devices: none -> 17.6 us  [rotated_exchange(): lax.ppermute(sent, axis, [(d, (d + far) % ways) for d in range(ways)])]
    ppermute x0 -> x7, starting transfers between devices: none -> 9.4 us  [rotated_exchange(): lax.ppermute(sent, axis, [(d, (d + far) % ways) for d in range(ways)])]
    all_to_all x1 -> x0, starting transfers between devices: 5.52 us -> none  [on_device(): lax.all_to_all(outgoing_rows, 'state', split_axis=1, concat_axis=1, tiled...]
  transfers between devices with their start and end apart: 4 -> 10, of which waited for: 4 -> 8; matrix products, arithmetic and copies ran while one was open for 3% -> 3% of each run, Pallas kernels for 0% -> 0%
where the time goes in v1:
time: 459 us; the launch traced here: 451 us
  matrix products  229 us (50%)
  waiting for transfers between devices  63.3 us (14%)
  local copies, waits for them, and re-layouts  56.2 us (12%)
  other arithmetic  43.7 us (10%)
  loops' own time  19 us (4%)
  starting transfers between devices  17.5 us (4%)
  between operations  16.4 us (4%)
  blocking collectives  5.78 us (1%)
    sub x32, matrix products, probabilities(): exp_scores = jnp.exp(scores - row_max)  40.1 us
    dot_general x16, matrix products, backward_block(): jnp.einsum('rhjk,rjhd->rkhd', weights_b, grad_blk, preferred_element_type...  32.6 us
    dot_general x16, matrix products, forward_block(): jnp.einsum('rhjk,rkhd->rjhd', weights_b, value_blk, preferred_element_typ...  27.8 us
    dot_general x16, matrix products, backward_block(): jnp.einsum('rhjk,rjhd->rkhd', score_b, query_blk, preferred_element_type=...  27.4 us
    dot_general x16, matrix products, backward_block(): jnp.einsum('rhjk,rkhd->rjhd', score_b, key_blk, preferred_element_type=jn...  26.4 us
    unnamed x2, waiting for transfers between devices  26.4 us
    add x16, other arithmetic, backward_block(): bias_sum + jnp.sum(score_grad, axis=0)  25.8 us
    dot_general x16, matrix products, backward_block(): jnp.einsum('rjhd,rkhd->rhjk', grad_blk, value_blk, preferred_element_type...  18.7 us
  transfers between devices with their start and end apart: 10, of which 8 were waited for; matrix products, arithmetic and copies ran while one was open for 3% of the time, Pallas kernels for 0%

profile of v1, /device:TPU:0, one launch (start us, length us, event | category | flops | bytes accessed | tf_op | source)
XLA Modules:
  0.0 450.9 jit_solution(7825938359700371691)
XLA Ops:
  6.5 4.4 all-to-all-start
  10.9 14.4 %all-to-all-done = bf16[4,16,64,128]{3,2,1,0:T(8,128)(2,1)S(1)} async-done(((bf16[4,16,64,128]{3,2,1,0:T(8,128)(2,1)}), bf16[4,16,64,128]{3,2,1,0:T(8,128)(2,1)S(1)}, u32[]{:S(2)}, u32[]{:S(2)}) %all-to-all-start) | async-done | bytes 1048608 | tf_op jit(solution)/shard_map/all_to_all | solution.py:73
  28.0 3.2 fusion.100
  31.2 5.8 %all_gather.3 = f32[4,128,128]{2,0,1:T(4,128)S(1)} all-gather(f32[4,32,128]{2,0,1:T(4,128)S(1)} %fusion.100), channel_id=1, replica_groups=mesh['state'=8,'tile'=4] {'tile'}, dimensions={1}, use_global_device_ids=true | all-gather | bytes 327680 | tf_op jit(solution)/shard_map/all_gather | solution.py:92
  41.0 2.7 reshape_reshape.15
  43.7 2.6 copy.162
  50.0 2.6 reshape_reshape.16
  52.6 2.7 copy.163
  59.7 2.6 copy.164
  62.3 68.6 %while.46 = (s32[]{:T(128)}, f32[16,2,128,4,32]{2,4,3,1,0:T(8,128)}, bf16[16,2,128,4,32]{2,4,3,1,0:T(8,128)(2,1)}, bf16[16,2,128,4,32]{2,4,3,1,0:T(8,128)(2,1)},...) while((s32[]{:T(128)}, f32[16,2,128,4,32]{2,4,3,1,0:T(8,128)}, ...), condition=%wide.region_5.6_spmd.clone, body=%wide.region_2.5_spmd.sunk.clone | while | flops 26346752 | bytes 3091525 | solution.py:106
  131.0 4.5 %copy.165 = f32[16,2,128,4,32]{2,1,0,4,3:T(2,128)} copy(f32[16,2,128,4,32]{2,4,3,1,0:T(8,128)} %get-tuple-element.226) | data formatting | bytes 4194304 | tf_op jit(solution)/shard_map/while | solution.py:106
  135.5 3.9 reshape.172
  139.4 3.0 copy.166
  142.4 3.7 multiply_convert_fusion.2
  149.0 2.8 copy.167
  151.7 3.5 all-to-all-start.1
  161.9 2.9 copy.170
  164.8 4.9 %all-to-all-done.1 = bf16[16,2,2,4,2048]{4,0,2,1,3:T(8,128)(2,1)S(1)} async-done(((bf16[16,2,2,4,2048]{4,0,2,1,3:T(8,128)(2,1)}), bf16[16,2,2,4,2048]{4,0,2,1,3:T(8,128)(2,1)S(1)}, u32[]{:S(2)}, u32[]{:S(2)}) %all-to-all-start.1) | async-done | bytes 1048608 | tf_op jit(solution)/shard_map/all_to_all | solution.py:120
  171.9 2.4 fusion.97
  175.8 3.5 fusion.110
  179.3 2.3 multiply_convert_fusion.1
  181.6 155.2 %while.48 = (s32[]{:T(128)}, f32[4,128,128]{1,2,0:T(8,128)}, bf16[16,2,128,4,32]{2,4,3,1,0:T(8,128)(2,1)}, bf16[16,2,128,4,32]{2,4,3,1,0:T(8,128)(2,1)}, bf16[16...) while((s32[]{:T(128)}, f32[4,128,128]{1,2,0:T(8,128)}, ...), condition=%wide.region_13.14_spmd.clone.clone, body=%wide.region_8.13_spmd.clone.sunk.clone | while | flops 52691200 | bytes 6518895 | solution.py:171
  336.9 3.1 fusion.124
  342.9 4.8 %fusion.103 = f32[32,128,128]{2,1,0:T(8,128)} fusion(f32[32,128,128]{1,2,0:T(8,128)} %copy.170, f32[32,128,128]{1,2,0:T(8,128)} %get-tuple-element.449, f32[32,128,128]{1,2,0:T(8,128)} %bitcast.299, bf16[128,128]{1,0:T(8,128)(2,1)S(1)} %copy-done.19), kind=kOutput, calls=%fused_computation.114 | convolution fusion | flops 136839168 | bytes 8421376 | tf_op jit(solution)/shard_map/rlw,cw->rlc/dot_general | solution.py:187
  349.5 26.4 %all-reduce.3.cloned.1.call-done = bf16[4,128,128]{2,0,1:T(4,128)(2,1)} async-done(((bf16[4,128,128]{2,0,1:T(4,128)(2,1)}), bf16[4,128,128]{2,0,1:T(4,128)(2,1)}) %all-reduce.3.cloned.1.call-update) | async-done | bytes 131088
  375.8 5.9 %fusion.139 = (f32[32,128]{1,0:T(8,128)S(1)}, f32[32,128]{1,0:T(8,128)S(1)}, f32[32,128,128]{2,1,0:T(8,128)S(1)}) fusion(f32[32,128]{1,0:T(8,128)S(1)} %rsqrt.17, f32[32,128,128]{2,1,0:T(8,128)S(1)} %bitcast.290, f32[32,128]{1,0:T(8,128)S(1)} %div.57, f32[128]{0:T(128)S(1)} %copy-done.21, f32[128,4]{0,1:T(4,128)S(1)} %copy-done.20, ...), kind=kOutput, calls=%fused_computation.165 | convolution fusion | flops 30400512 | bytes 12683780 | tf_op jit(solution)/shard_map/hrl,ch->rlc/dot_general | solution.py:200
  381.7 2.5 add_convert_fusion
  385.6 4.3 collective-permute-start
  390.4 2.9 collective-permute-start.3
  396.6 2.7 collective-permute-done.2
  399.4 11.9 %collective-permute-done.3 = bf16[32,1,16,128]{3,2,1,0:T(8,128)(2,1)S(1)} collective-permute-done((bf16[32,1,16,128]{3,2,1,0:T(8,128)(2,1)S(1)}, bf16[32,1,16,128]{3,2,1,0:T(8,128)(2,1)S(1)}, u32[]{:S(2)}, u32[]{:S(2)}) %collective-permute-start.3) | collective-permute-done | bytes 131104 | tf_op jit(solution)/shard_map/ppermute | solution.py:21
  413.6 29.5 %while.47 = (s32[]{:T(128)}, f32[4,16,2,16,128]{4,3,2,1,0:T(8,128)S(1)}, s32[8]{0:T(128)S(1)}, f32[8,2,16,16,128]{4,3,0,1,2:T(8,128)S(1)}, s32[]{:T(128)}) while((s32[]{:T(128)}, f32[4,16,2,16,128]{4,3,2,1,0:T(8,128)S(1)}, s32[8]{0:T(128)S(1)}, f32[8,2,16,16,128]{4,3,0,1,2:T(8,128)S(1)}, s32[]{:T(128)}) %tuple.146), condition=%wide.region_18.20_spmd.clone.clone, body=%wide.region_17.19_spmd.clone.sunk.clone | while | flops 393300 | bytes 2360721 | solution.py:234
  (345 shorter events, 272.6 us)
Async XLA Ops:
  6.5 139.6 %copy-start = (bf16[128,128]{1,0:T(8,128)(2,1)S(1)}, bf16[128,128]{1,0:T(8,128)(2,1)}, u32[]{:S(2)}) copy-start(bf16[128,128]{1,0:T(8,128)(2,1)} %param.34) | copy-start | bytes 98308
  6.5 18.8 %all-to-all-start = ((bf16[4,16,64,128]{3,2,1,0:T(8,128)(2,1)}), bf16[4,16,64,128]{3,2,1,0:T(8,128)(2,1)S(1)}, u32[]{:S(2)}, u32[]{:S(2)}) async-start(bf16[4,16,64,128]{3,2,1,0:T(8,128)(2,1)} %bitcast.308), calls=%async_computation | async-start | bytes 2097152 | tf_op jit(solution)/shard_map/all_to_all | solution.py:73
  26.1 1.9 copy-start.20
  26.1 1.9 copy-start.21
  26.1 1.9 copy-start.22
  28.0 11.3 %copy-start.14 = (bf16[128,128]{1,0:T(8,128)(2,1)S(1)}, bf16[128,128]{1,0:T(8,128)(2,1)}, u32[]{:S(2)}) copy-start(bf16[128,128]{1,0:T(8,128)(2,1)} %param.30) | copy-start | bytes 98308
  41.0 5.3 %copy-start.6 = (bf16[4096,128]{1,0:T(8,128)(2,1)S(1)}, bf16[4096,128]{1,0:T(8,128)(2,1)}, u32[]{:S(2)}) copy-start(bf16[4096,128]{1,0:T(8,128)(2,1)} %copy-done.5) | copy-start | bytes 3145732
  41.0 5.3 %copy-start.16 = (bf16[128,128]{1,0:T(8,128)(2,1)S(1)}, bf16[128,128]{1,0:T(8,128)(2,1)}, u32[]{:S(2)}) copy-start(bf16[128,128]{1,0:T(8,128)(2,1)} %param.28) | copy-start | bytes 98308
  50.0 5.3 %copy-start.15 = (bf16[128,128]{1,0:T(8,128)(2,1)S(1)}, bf16[128,128]{1,0:T(8,128)(2,1)}, u32[]{:S(2)}) copy-start(bf16[128,128]{1,0:T(8,128)(2,1)} %param.29) | copy-start | bytes 98308
  139.4 3.0 copy-start.7
  139.4 3.0 copy-start.26
  142.4 3.7 copy-start.23
  151.7 17.9 %all-to-all-start.1 = ((bf16[16,2,2,4,2048]{4,0,2,1,3:T(8,128)(2,1)}), bf16[16,2,2,4,2048]{4,0,2,1,3:T(8,128)(2,1)S(1)}, u32[]{:S(2)}, u32[]{:S(2)}) async-start(bf16[16,2,2,4,2048]{4,0,2,1,3:T(8,128)(2,1)} %copy.167), calls=%async_computation.1 | async-start | bytes 2097152 | tf_op jit(solution)/shard_map/all_to_all | solution.py:120
  155.3 220.5 %all-reduce.3.cloned.1.call-start = ((), (), s32[]{:S(2)}) async-start(), calls=%async_computation.2 | async-start | bytes 262144
  155.7 2.4 copy-start.27
  155.8 4.9 %copy-start.28 = (u32[32]{0:T(128)S(1)}, u32[32]{0:T(128)}, u32[]{:S(2)}) copy-start(u32[32]{0:T(128)} %constant.201) | copy-start | bytes 388
  170.3 1.6 copy-start.12
  175.8 3.5 copy-start.2
  179.3 2.3 copy-start.10
  336.8 3.2 copy-start.13
  340.0 1.8 copy-start.9
  340.0 2.9 copy-start.19
  342.9 4.8 %copy-start.4 = (bf16[16,2,128,4,32]{2,4,3,1,0:T(8,128)(2,1)S(1)}, bf16[16,2,128,4,32]{2,4,3,1,0:T(8,128)(2,1)}, u32[]{:S(2)}) copy-start(bf16[16,2,128,4,32]{2,4,3,1,0:T(8,128)(2,1)} %get-tuple-element.227) | copy-start | bytes 3145732
  342.9 4.8 %copy-start.17 = (bf16[128,128]{1,0:T(8,128)(2,1)S(1)}, bf16[128,128]{1,0:T(8,128)(2,1)}, u32[]{:S(2)}) copy-start(bf16[128,128]{1,0:T(8,128)(2,1)} %param.28) | copy-start | bytes 98308
  375.8 5.9 %copy-start.11 = (f32[32,128,128]{2,1,0:T(8,128)S(1)}, f32[32,128,128]{2,1,0:T(8,128)}, u32[]{:S(2)}) copy-start(f32[32,128,128]{2,1,0:T(8,128)} %copy-done.10) | copy-start | bytes 6291460
  385.6 8.2 %collective-permute-start = (bf16[32,1,16,128]{3,2,1,0:T(8,128)(2,1)S(1)}, bf16[32,1,16,128]{3,2,1,0:T(8,128)(2,1)S(1)}, u32[]{:S(2)}, u32[]{:S(2)}) collective-permute-start(bf16[32,1,16,128]{3,2,1,0:T(8,128)(2,1)S(1)} %get-tuple-element.441), channel_id=1, source_target_pairs={{0,28},{4,0},{8,4},{12,8},{16,12},{20,16},{24,20},{28,24},{1,29},{... | collective-permute-start | bytes 393224 | tf_op jit(solution)/shard_map/ppermute | solution.py:21
  389.9 6.7 %collective-permute-start.1 = (bf16[32,1,16,128]{3,2,1,0:T(8,128)(2,1)S(1)}, bf16[32,1,16,128]{3,2,1,0:T(8,128)(2,1)S(1)}, u32[]{:S(2)}, u32[]{:S(2)}) collective-permute-start(bf16[32,1,16,128]{3,2,1,0:T(8,128)(2,1)S(1)} %get-tuple-element.440), channel_id=1, source_target_pairs={{0,24},{4,28},{8,0},{12,4},{16,8},{20,12},{24,16},{28,20},{1,25},{... | collective-permute-start | bytes 393224 | tf_op jit(solution)/shard_map/ppermute | solution.py:21
  390.4 9.0 %collective-permute-start.2 = (bf16[32,1,16,128]{3,2,1,0:T(8,128)(2,1)S(1)}, bf16[32,1,16,128]{3,2,1,0:T(8,128)(2,1)S(1)}, u32[]{:S(2)}, u32[]{:S(2)}) collective-permute-start(bf16[32,1,16,128]{3,2,1,0:T(8,128)(2,1)S(1)} %get-tuple-element.439), channel_id=1, source_target_pairs={{0,20},{4,24},{8,28},{12,0},{16,4},{20,8},{24,12},{28,16},{1,21},{... | collective-permute-start | bytes 393224 | tf_op jit(solution)/shard_map/ppermute | solution.py:21
  390.4 20.9 %collective-permute-start.3 = (bf16[32,1,16,128]{3,2,1,0:T(8,128)(2,1)S(1)}, bf16[32,1,16,128]{3,2,1,0:T(8,128)(2,1)S(1)}, u32[]{:S(2)}, u32[]{:S(2)}) collective-permute-start(bf16[32,1,16,128]{3,2,1,0:T(8,128)(2,1)S(1)} %get-tuple-element.438), channel_id=1, source_target_pairs={{0,16},{4,20},{8,24},{12,28},{16,0},{20,4},{24,8},{28,12},{1,17},{... | collective-permute-start | bytes 393224 | tf_op jit(solution)/shard_map/ppermute | solution.py:21
  393.3 19.3 %collective-permute-start.4 = (bf16[32,1,16,128]{3,2,1,0:T(8,128)(2,1)S(1)}, bf16[32,1,16,128]{3,2,1,0:T(8,128)(2,1)S(1)}, u32[]{:S(2)}, u32[]{:S(2)}) collective-permute-start(bf16[32,1,16,128]{3,2,1,0:T(8,128)(2,1)S(1)} %get-tuple-element.437), channel_id=1, source_target_pairs={{0,12},{4,16},{8,20},{12,24},{16,28},{20,0},{24,4},{28,8},{1,13},{... | collective-permute-start | bytes 393224 | tf_op jit(solution)/shard_map/ppermute | solution.py:21
  393.8 19.0 %collective-permute-start.5 = (bf16[32,1,16,128]{3,2,1,0:T(8,128)(2,1)S(1)}, bf16[32,1,16,128]{3,2,1,0:T(8,128)(2,1)S(1)}, u32[]{:S(2)}, u32[]{:S(2)}) collective-permute-start(bf16[32,1,16,128]{3,2,1,0:T(8,128)(2,1)S(1)} %get-tuple-element.436), channel_id=1, source_target_pairs={{0,8},{4,12},{8,16},{12,20},{16,24},{20,28},{24,0},{28,4},{1,9},{5... | collective-permute-start | bytes 393224 | tf_op jit(solution)/shard_map/ppermute | solution.py:21
  396.6 16.2 %collective-permute-start.6 = (bf16[32,1,16,128]{3,2,1,0:T(8,128)(2,1)S(1)}, bf16[32,1,16,128]{3,2,1,0:T(8,128)(2,1)S(1)}, u32[]{:S(2)}, u32[]{:S(2)}) collective-permute-start(bf16[32,1,16,128]{3,2,1,0:T(8,128)(2,1)S(1)} %get-tuple-element.435), channel_id=1, source_target_pairs={{0,4},{4,8},{8,12},{12,16},{16,20},{20,24},{24,28},{28,0},{1,5},{5... | collective-permute-start | bytes 393224 | tf_op jit(solution)/shard_map/ppermute | solution.py:21
  (7 other events, 8.9 us)
Sparse Core Ops, SparseCore 0:
  343.0 32.7 all-reduce.2
